TPU v7x, 32 devices: a whole 2x2x4 slice. The times are simulated.
32 devices in a mesh: domain: 2 (over x), fsdp: 16 (over z, y, core).
Axes of the slice: x: 2, y: 2, z: 4, core: 2. Of those that a mesh axis runs over, the one named last changes fastest.
Arguments:
- gradients: bfloat16 [2, 4, 4096, 512], P('domain', None, 'fsdp')
- row_counts: int32 [4], replicated, may hold values from 2048 to 4096, as said below
- domain_ids: int32 [2], replicated, may hold values from 0 to 7
- domain_weights: float32 [8], replicated, may hold values from 0.2 to 2
Outputs:
- updates: float32 [4, 4096, 512], P('domain', 'fsdp')
- new_weights: float32 [8], replicated
Inputs may be any that keep to these rules, and one draw needn't show every extreme that they name: `row_counts`: each matrix has 4096 or 2048 rows, and both counts occur.
All inputs are finite; a program needn't handle non-finite values.
Results may differ from a plain program's by a relative error of at most 0.0071.
Values may be sent and summed in bfloat16 or wider, within the bound.
No kernel may reach another device: no remote copies, remote signals or barrier semaphores. Data moves between devices by JAX's collectives and lax.ppermute only.
A program may use at most 64 MiB of HBM per device.

v0:
```python
import math
import jax
import jax.numpy as jnp
from jax import lax
from jax.sharding import PartitionSpec as P

NS_ITERS = 3
OWNERS = 8
COEF_A = 3.4445
COEF_B = -4.775
COEF_C = 2.0315
MUON_SCALE = 0.2
ETA = 4.0


def partner(shard, axis, stride):
    return lax.ppermute(shard, axis, [(i, i ^ 1 << stride) for i in range(lax.axis_size(axis))])


def group_mixing(domain_ids, domain_weights, kind_count):
    weight_share = domain_weights / jnp.sum(domain_weights)
    onehot = (domain_ids[:, None] == jnp.arange(kind_count, dtype=jnp.int32)[None, :]).astype(
        jnp.float32
    )
    counts = jnp.sum(onehot, axis=0)
    per_member = weight_share / jnp.maximum(counts, 1.0)
    group_mix = jnp.sum(onehot * per_member[None, :], axis=1)
    return (weight_share, onehot, counts, group_mix)


def summed_gram(iterate):
    gram_total = lax.dot_general(
        iterate, iterate, (((0,), (0,)), ((), ())), preferred_element_type=jnp.float32
    )
    for bit_pos in range(OWNERS.bit_length() - 1):
        gram_total = gram_total + partner(gram_total, "fsdp", bit_pos)
    return gram_total


def newton_steps(iterate):
    for repeat in range(NS_ITERS):
        gram_full = lax.optimization_barrier(summed_gram(iterate).astype(jnp.bfloat16))
        square = jnp.dot(gram_full, gram_full, preferred_element_type=jnp.float32)
        poly_term = (COEF_B * gram_full.astype(jnp.float32) + COEF_C * square).astype(jnp.bfloat16)
        iterate = lax.optimization_barrier(
            (
                COEF_A * iterate.astype(jnp.float32)
                + jnp.dot(iterate, poly_term, preferred_element_type=jnp.float32)
            ).astype(jnp.bfloat16)
        )
    return iterate


def share_scores(aligned, squares, norm_slots):
    return lax.psum((aligned, squares, norm_slots), ("domain", "fsdp"))


def body(gradients, row_counts, domain_ids, domain_weights):
    groups = lax.axis_size("domain")
    shards = lax.axis_size("fsdp")
    matrices = row_counts.shape[0]
    rows_src = gradients.shape[2]
    columns = gradients.shape[3]
    per_domain = matrices // groups
    sub_rows = rows_src // OWNERS
    own_rows = shards * sub_rows
    full_rows = rows_src * shards
    domain_pos = lax.axis_index("domain")
    shard_pos = lax.axis_index("fsdp")
    weight_share, onehot, counts, group_mix = group_mixing(
        domain_ids, domain_weights, domain_weights.shape[0]
    )
    blocks = lax.all_to_all(
        gradients.reshape(1, groups, per_domain, rows_src, columns),
        "domain",
        split_axis=1,
        concat_axis=0,
        tiled=True,
    )
    blocks = blocks.reshape(groups, per_domain, rows_src, columns)
    global_rows = shard_pos * rows_src + jnp.arange(rows_src, dtype=jnp.int32)
    limits = lax.dynamic_slice_in_dim(row_counts, domain_pos * per_domain, per_domain, 0)
    row_mask = (global_rows[None, :] < limits[:, None])[None, :, :, None]
    masked = jnp.where(row_mask, blocks.astype(jnp.float32), jnp.zeros((), jnp.float32))
    combined = jnp.sum(group_mix[:, None, None, None] * masked, axis=0)
    aligned = jnp.sum(masked * combined[None], axis=(1, 2, 3))
    squares = jnp.sum(masked * masked, axis=(1, 2, 3))
    block_squares = jnp.sum(combined * combined, axis=(1, 2))
    norm_slots = lax.dynamic_update_slice_in_dim(
        jnp.zeros((matrices,), jnp.float32), block_squares, domain_pos * per_domain, 0
    )
    aligned, squares, norm_slots = share_scores(aligned, squares, norm_slots)
    frob_norm = (
        jnp.sqrt(lax.dynamic_slice_in_dim(norm_slots, domain_pos * per_domain, per_domain, 0))
        + 1e-07
    )
    scaled = (combined / frob_norm[:, None, None]).astype(jnp.bfloat16)
    scaled = scaled.reshape(shards, 1, sub_rows, columns)
    start_rows = lax.all_to_all(scaled, "fsdp", split_axis=0, concat_axis=1, tiled=True)
    start_rows = lax.optimization_barrier(start_rows.reshape(own_rows, columns))
    finished = newton_steps(start_rows)
    returned = lax.all_to_all(
        finished.reshape(1, shards, sub_rows, columns),
        "fsdp",
        split_axis=1,
        concat_axis=0,
        tiled=True,
    )
    returned = returned.reshape(per_domain, rows_src, columns)
    updates = returned.astype(jnp.float32) * (MUON_SCALE * math.sqrt(full_rows))
    total_sq = jnp.sum(norm_slots)
    cosine = aligned / (jnp.sqrt(squares) * jnp.sqrt(total_sq) + 1e-06)
    score = jnp.sum(onehot * cosine[:, None], axis=0) / jnp.maximum(counts, 1.0)
    raised = weight_share * jnp.exp(ETA * score)
    return (updates, raised / jnp.sum(raised))


def solution(mesh):
    placed = (P("domain", None, "fsdp", None), P(), P(), P())
    return jax.shard_map(
        body,
        mesh=mesh,
        in_specs=placed,
        out_specs=(P("domain", "fsdp", None), P()),
        check_vma=False,
    )
```

profile of v0, /device:TPU:0, one launch (start us, length us, event | category | flops | bytes accessed | tf_op | source)
XLA Modules:
  0.0 265.7 jit_solution(6877497156156330844)
XLA Ops:
  0.7 4.4 %all-to-all-start = ((bf16[1,2,2,256,512]{4,3,2,0,1:T(8,128)(2,1)}), bf16[1,2,2,256,512]{4,3,2,0,1:T(8,128)(2,1)S(1)}, u32[]{:S(2)}, u32[]{:S(2)}) async-start(bf16[1,2,2,256,512]{4,3,2,0,1:T(8,128)(2,1)} %bitcast.31), calls=%async_computation | async-start | bytes 2097152 | tf_op jit(solution)/shard_map/all_to_all | solution.py:73
  6.7 12.7 %all-to-all-done = bf16[1,2,2,256,512]{4,3,2,0,1:T(8,128)(2,1)S(1)} async-done(((bf16[1,2,2,256,512]{4,3,2,0,1:T(8,128)(2,1)}), bf16[1,2,2,256,512]{4,3,2,0,1:T(8,128)(2,1)S(1)}, u32[]{:S(2)}, u32[]{:S(2)}) %all-to-all-start) | async-done | bytes 1048608 | tf_op jit(solution)/shard_map/all_to_all | solution.py:73
  20.9 39.8 %all-reduce = (f32[4]{0:T(128)S(1)}, f32[2]{0:T(128)S(1)}, f32[2]{0:T(128)S(1)}) all-reduce(f32[4]{0:T(128)S(1)} %dynamic_update_slice.3, f32[2]{0:T(128)S(1)} %get-tuple-element.3, f32[2]{0:T(128)S(1)} %get-tuple-element.2), channel_id=1, replica_groups=mesh['domain'=2,'fsdp'=16] {'domain','fsdp'}, use_global_device_ids=true, to_apply=%region_5.6 | all-reduce | flops 8 | bytes 64 | tf_op jit(solution)/shard_map/psum | solution.py:55
  62.4 19.5 %all_to_all.12 = bf16[16,1,32,512]{3,2,1,0:T(8,128)(2,1)S(1)} all-to-all(bf16[16,1,32,512]{3,2,1,0:T(8,128)(2,1)S(1)} %divide_convert_fusion), channel_id=1, replica_groups=mesh['domain'=2,'fsdp'=16] {'fsdp'}, dimensions={0} | all-to-all | bytes 1048576 | tf_op jit(solution)/shard_map/all_to_all | solution.py:99
  82.6 2.5 collective-permute-done
  86.4 24.2 %collective-permute-done.1 = f32[512,512]{1,0:T(8,128)S(1)} collective-permute-done((f32[512,512]{1,0:T(8,128)S(1)}, f32[512,512]{1,0:T(8,128)S(1)}, u32[]{:S(2)}, u32[]{:S(2)}) %collective-permute-start.1) | collective-permute-done | bytes 1048608 | tf_op jit(solution)/shard_map/ppermute | solution.py:17
  110.8 1.8 collective-permute-start.2
  112.6 22.8 %collective-permute-done.2 = f32[512,512]{1,0:T(8,128)S(1)} collective-permute-done((f32[512,512]{1,0:T(8,128)S(1)}, f32[512,512]{1,0:T(8,128)S(1)}, u32[]{:S(2)}, u32[]{:S(2)}) %collective-permute-start.2) | collective-permute-done | bytes 1048608 | tf_op jit(solution)/shard_map/ppermute | solution.py:17
  137.0 2.6 collective-permute-done.3
  139.9 1.3 collective-permute-start.4
  141.2 23.9 %collective-permute-done.4 = f32[512,512]{1,0:T(8,128)S(1)} collective-permute-done((f32[512,512]{1,0:T(8,128)S(1)}, f32[512,512]{1,0:T(8,128)S(1)}, u32[]{:S(2)}, u32[]{:S(2)}) %collective-permute-start.4) | collective-permute-done | bytes 1048608 | tf_op jit(solution)/shard_map/ppermute | solution.py:17
  165.4 1.8 collective-permute-start.5
  167.2 22.6 %collective-permute-done.5 = f32[512,512]{1,0:T(8,128)S(1)} collective-permute-done((f32[512,512]{1,0:T(8,128)S(1)}, f32[512,512]{1,0:T(8,128)S(1)}, u32[]{:S(2)}, u32[]{:S(2)}) %collective-permute-start.5) | collective-permute-done | bytes 1048608 | tf_op jit(solution)/shard_map/ppermute | solution.py:17
  191.4 2.6 collective-permute-done.6
  194.2 1.3 collective-permute-start.7
  195.6 23.9 %collective-permute-done.7 = f32[512,512]{1,0:T(8,128)S(1)} collective-permute-done((f32[512,512]{1,0:T(8,128)S(1)}, f32[512,512]{1,0:T(8,128)S(1)}, u32[]{:S(2)}, u32[]{:S(2)}) %collective-permute-start.7) | collective-permute-done | bytes 1048608 | tf_op jit(solution)/shard_map/ppermute | solution.py:17
  219.7 1.8 collective-permute-start.8
  221.5 22.6 %collective-permute-done.8 = f32[512,512]{1,0:T(8,128)S(1)} collective-permute-done((f32[512,512]{1,0:T(8,128)S(1)}, f32[512,512]{1,0:T(8,128)S(1)}, u32[]{:S(2)}, u32[]{:S(2)}) %collective-permute-start.8) | collective-permute-done | bytes 1048608 | tf_op jit(solution)/shard_map/ppermute | solution.py:17
  244.4 1.6 fusion.8
  245.9 4.4 %all-to-all-start.2 = ((bf16[1,16,32,512]{3,2,0,1:T(8,128)(2,1)}), bf16[1,16,32,512]{3,2,0,1:T(8,128)(2,1)S(1)}, u32[]{:S(2)}, u32[]{:S(2)}) async-start(bf16[1,16,32,512]{3,2,0,1:T(8,128)(2,1)} %bitcast.5), calls=%async_computation.2 | async-start | bytes 1048576 | tf_op jit(solution)/shard_map/all_to_all | solution.py:102
  250.4 1.3 fusion.21
  251.8 1.2 broadcast_divide_fusion
  253.0 11.6 %all-to-all-done.2 = bf16[1,16,32,512]{3,2,0,1:T(8,128)(2,1)S(1)} async-done(((bf16[1,16,32,512]{3,2,0,1:T(8,128)(2,1)}), bf16[1,16,32,512]{3,2,0,1:T(8,128)(2,1)S(1)}, u32[]{:S(2)}, u32[]{:S(2)}) %all-to-all-start.2) | async-done | bytes 524320 | tf_op jit(solution)/shard_map/all_to_all | solution.py:102
  264.6 1.1 convert_multiply_fusion
  (42 shorter events, 10.6 us)
Async XLA Ops:
  0.6 4.4 %copy-start.2 = (s32[2]{0:T(128)S(1)}, s32[2]{0:T(128)}, u32[]{:S(2)}) copy-start(s32[2]{0:T(128)} %param.6) | copy-start | bytes 28
  0.6 4.5 %copy-start = (f32[8]{0:T(128)S(1)}, f32[8]{0:T(128)}, u32[]{:S(2)}) copy-start(f32[8]{0:T(128)} %param.7) | copy-start | bytes 100
  0.7 5.1 %copy-start.1 = (s32[4]{0:T(128)S(1)}, s32[4]{0:T(128)}, u32[]{:S(2)}) copy-start(s32[4]{0:T(128)} %param.5) | copy-start | bytes 52
  0.7 18.8 %all-to-all-start = ((bf16[1,2,2,256,512]{4,3,2,0,1:T(8,128)(2,1)}), bf16[1,2,2,256,512]{4,3,2,0,1:T(8,128)(2,1)S(1)}, u32[]{:S(2)}, u32[]{:S(2)}) async-start(bf16[1,2,2,256,512]{4,3,2,0,1:T(8,128)(2,1)} %bitcast.31), calls=%async_computation | async-start | bytes 2097152 | tf_op jit(solution)/shard_map/all_to_all | solution.py:73
  82.4 2.7 %collective-permute-start = (f32[512,512]{1,0:T(8,128)S(1)}, f32[512,512]{1,0:T(8,128)S(1)}, u32[]{:S(2)}, u32[]{:S(2)}) collective-permute-start(f32[512,512]{1,0:T(8,128)S(1)} %fusion.22), channel_id=1, source_target_pairs={{0,1},{1,0},{2,3},{3,2},{4,5},{5,4},{6,7},{7,6},{8,9},{9,8},{10,11... | collective-permute-start | bytes 3145736 | tf_op jit(solution)/shard_map/ppermute | solution.py:17
  85.3 25.3 %collective-permute-start.1 = (f32[512,512]{1,0:T(8,128)S(1)}, f32[512,512]{1,0:T(8,128)S(1)}, u32[]{:S(2)}, u32[]{:S(2)}) collective-permute-start(f32[512,512]{1,0:T(8,128)S(1)} %add.76), channel_id=1, source_target_pairs={{0,2},{1,3},{2,0},{3,1},{4,6},{5,7},{6,4},{7,5},{8,10},{9,11},{10,... | collective-permute-start | bytes 3145736 | tf_op jit(solution)/shard_map/ppermute | solution.py:17
  110.8 24.7 %collective-permute-start.2 = (f32[512,512]{1,0:T(8,128)S(1)}, f32[512,512]{1,0:T(8,128)S(1)}, u32[]{:S(2)}, u32[]{:S(2)}) collective-permute-start(f32[512,512]{1,0:T(8,128)S(1)} %add.77), channel_id=1, source_target_pairs={{0,4},{1,5},{2,6},{3,7},{4,0},{5,1},{6,2},{7,3},{8,12},{9,13},{10,... | collective-permute-start | bytes 3145736 | tf_op jit(solution)/shard_map/ppermute | solution.py:17
  137.0 2.7 %collective-permute-start.3 = (f32[512,512]{1,0:T(8,128)S(1)}, f32[512,512]{1,0:T(8,128)S(1)}, u32[]{:S(2)}, u32[]{:S(2)}) collective-permute-start(f32[512,512]{1,0:T(8,128)S(1)} %fusion.23), channel_id=1, source_target_pairs={{0,1},{1,0},{2,3},{3,2},{4,5},{5,4},{6,7},{7,6},{8,9},{9,8},{10,11... | collective-permute-start | bytes 3145736 | tf_op jit(solution)/shard_map/ppermute | solution.py:17
  139.9 25.3 %collective-permute-start.4 = (f32[512,512]{1,0:T(8,128)S(1)}, f32[512,512]{1,0:T(8,128)S(1)}, u32[]{:S(2)}, u32[]{:S(2)}) collective-permute-start(f32[512,512]{1,0:T(8,128)S(1)} %add.81), channel_id=1, source_target_pairs={{0,2},{1,3},{2,0},{3,1},{4,6},{5,7},{6,4},{7,5},{8,10},{9,11},{10,... | collective-permute-start | bytes 3145736 | tf_op jit(solution)/shard_map/ppermute | solution.py:17
  165.4 24.4 %collective-permute-start.5 = (f32[512,512]{1,0:T(8,128)S(1)}, f32[512,512]{1,0:T(8,128)S(1)}, u32[]{:S(2)}, u32[]{:S(2)}) collective-permute-start(f32[512,512]{1,0:T(8,128)S(1)} %add.82), channel_id=1, source_target_pairs={{0,4},{1,5},{2,6},{3,7},{4,0},{5,1},{6,2},{7,3},{8,12},{9,13},{10,... | collective-permute-start | bytes 3145736 | tf_op jit(solution)/shard_map/ppermute | solution.py:17
  191.3 2.7 %collective-permute-start.6 = (f32[512,512]{1,0:T(8,128)S(1)}, f32[512,512]{1,0:T(8,128)S(1)}, u32[]{:S(2)}, u32[]{:S(2)}) collective-permute-start(f32[512,512]{1,0:T(8,128)S(1)} %fusion.24), channel_id=1, source_target_pairs={{0,1},{1,0},{2,3},{3,2},{4,5},{5,4},{6,7},{7,6},{8,9},{9,8},{10,11... | collective-permute-start | bytes 3145736 | tf_op jit(solution)/shard_map/ppermute | solution.py:17
  194.2 25.3 %collective-permute-start.7 = (f32[512,512]{1,0:T(8,128)S(1)}, f32[512,512]{1,0:T(8,128)S(1)}, u32[]{:S(2)}, u32[]{:S(2)}) collective-permute-start(f32[512,512]{1,0:T(8,128)S(1)} %add.86), channel_id=1, source_target_pairs={{0,2},{1,3},{2,0},{3,1},{4,6},{5,7},{6,4},{7,5},{8,10},{9,11},{10,... | collective-permute-start | bytes 3145736 | tf_op jit(solution)/shard_map/ppermute | solution.py:17
  219.7 24.4 %collective-permute-start.8 = (f32[512,512]{1,0:T(8,128)S(1)}, f32[512,512]{1,0:T(8,128)S(1)}, u32[]{:S(2)}, u32[]{:S(2)}) collective-permute-start(f32[512,512]{1,0:T(8,128)S(1)} %add.87), channel_id=1, source_target_pairs={{0,4},{1,5},{2,6},{3,7},{4,0},{5,1},{6,2},{7,3},{8,12},{9,13},{10,... | collective-permute-start | bytes 3145736 | tf_op jit(solution)/shard_map/ppermute | solution.py:17
  245.9 18.7 %all-to-all-start.2 = ((bf16[1,16,32,512]{3,2,0,1:T(8,128)(2,1)}), bf16[1,16,32,512]{3,2,0,1:T(8,128)(2,1)S(1)}, u32[]{:S(2)}, u32[]{:S(2)}) async-start(bf16[1,16,32,512]{3,2,0,1:T(8,128)(2,1)} %bitcast.5), calls=%async_computation.2 | async-start | bytes 1048576 | tf_op jit(solution)/shard_map/all_to_all | solution.py:102
where the time goes:
time: 266 us
  waiting for transfers between devices  172 us (65%)
  blocking collectives  59.3 us (22%)
  starting transfers between devices  18.3 us (7%)
  other arithmetic  9.43 us (4%)
  matrix products  4.55 us (2%)
    ppermute x9, waiting for transfers between devices, partner(): lax.ppermute(shard, axis, [(i, i ^ 1 << stride) for i in range(lax.axis_s...  148 us
    psum x1, blocking collectives, share_scores(): return lax.psum((aligned, squares, norm_slots), ('domain', 'fsdp'))  39.8 us
    all_to_all x1, blocking collectives, body(): lax.all_to_all(scaled, 'fsdp', split_axis=0, concat_axis=1, tiled=True)  19.5 us
    all_to_all x1, waiting for transfers between devices, body(): lax.all_to_all(gradients.reshape(1, groups, per_domain, rows_src, columns...  12.7 us
    all_to_all x1, waiting for transfers between devices, body(): lax.all_to_all(finished.reshape(1, shards, sub_rows, columns), 'fsdp', sp...  11.6 us
    ppermute x9, starting transfers between devices, partner(): lax.ppermute(shard, axis, [(i, i ^ 1 << stride) for i in range(lax.axis_s...  9.5 us
  transfers between devices with their start and end apart: 11, of which 11 were waited for; matrix products, arithmetic and copies ran while one was open for 2% of the time, Pallas kernels for 0%

commit v1 on v0

--- a/solution.py
+++ b/solution.py
@@ -99,13 +99,11 @@
     start_rows = lax.all_to_all(scaled, "fsdp", split_axis=0, concat_axis=1, tiled=True)
     start_rows = lax.optimization_barrier(start_rows.reshape(own_rows, columns))
     finished = newton_steps(start_rows)
-    returned = lax.all_to_all(
-        finished.reshape(1, shards, sub_rows, columns),
-        "fsdp",
-        split_axis=1,
-        concat_axis=0,
-        tiled=True,
-    )
+    own = finished.reshape(1, shards, sub_rows, columns)
+    peers = lax.axis_size("fsdp")
+    tiles = jnp.stack(jnp.split(own, peers, axis=1), axis=0)
+    tiles = lax.all_to_all(tiles, "fsdp", split_axis=0, concat_axis=0)
+    returned = jnp.concatenate(tiles, axis=0)
     returned = returned.reshape(per_domain, rows_src, columns)
     updates = returned.astype(jnp.float32) * (MUON_SCALE * math.sqrt(full_rows))
     total_sq = jnp.sum(norm_slots)

time: 266 us -> 275 us (1.034)
  local copies, waits for them, and re-layouts: 0.45 us -> 10.3 us
    unnamed x6 -> x21, local copies, waits for them, and re-layouts: 0.01 us -> 9.27 us
where the time goes in v1:
time: 275 us
  waiting for transfers between devices  172 us (63%)
  blocking collectives  59.3 us (22%)
  starting transfers between devices  18.3 us (7%)
  local copies, waits for them, and re-layouts  10.3 us (4%)
  other arithmetic  9.43 us (3%)
  matrix products  3.76 us (1%)
    ppermute x9, waiting for transfers between devices, partner(): lax.ppermute(shard, axis, [(i, i ^ 1 << stride) for i in range(lax.axis_s...  148 us
    psum x1, blocking collectives, share_scores(): return lax.psum((aligned, squares, norm_slots), ('domain', 'fsdp'))  39.8 us
    all_to_all x1, blocking collectives, body(): lax.all_to_all(scaled, 'fsdp', split_axis=0, concat_axis=1, tiled=True)  19.5 us
    all_to_all x1, waiting for transfers between devices, body(): lax.all_to_all(gradients.reshape(1, groups, per_domain, rows_src, columns...  12.7 us
    all_to_all x1, waiting for transfers between devices, body(): tiles = lax.all_to_all(tiles, 'fsdp', split_axis=0, concat_axis=0)  11.6 us
    ppermute x9, starting transfers between devices, partner(): lax.ppermute(shard, axis, [(i, i ^ 1 << stride) for i in range(lax.axis_s...  9.5 us
    unnamed x21, local copies, waits for them, and re-layouts  9.27 us
  transfers between devices with their start and end apart: 11, of which 11 were waited for; matrix products, arithmetic and copies ran while one was open for 2% of the time, Pallas kernels for 0%

profile of v1, /device:TPU:0, one launch (start us, length us, event | category | flops | bytes accessed | tf_op | source)
XLA Modules:
  0.0 274.8 jit_solution(17265807208124331219)
XLA Ops:
  0.7 4.4 %all-to-all-start = ((bf16[1,2,2,256,512]{4,3,2,0,1:T(8,128)(2,1)}), bf16[1,2,2,256,512]{4,3,2,0,1:T(8,128)(2,1)S(1)}, u32[]{:S(2)}, u32[]{:S(2)}) async-start(bf16[1,2,2,256,512]{4,3,2,0,1:T(8,128)(2,1)} %bitcast.93), calls=%async_computation | async-start | bytes 2097152 | tf_op jit(solution)/shard_map/all_to_all | solution.py:73
  6.7 12.7 %all-to-all-done = bf16[1,2,2,256,512]{4,3,2,0,1:T(8,128)(2,1)S(1)} async-done(((bf16[1,2,2,256,512]{4,3,2,0,1:T(8,128)(2,1)}), bf16[1,2,2,256,512]{4,3,2,0,1:T(8,128)(2,1)S(1)}, u32[]{:S(2)}, u32[]{:S(2)}) %all-to-all-start) | async-done | bytes 1048608 | tf_op jit(solution)/shard_map/all_to_all | solution.py:73
  20.9 39.8 %all-reduce = (f32[4]{0:T(128)S(1)}, f32[2]{0:T(128)S(1)}, f32[2]{0:T(128)S(1)}) all-reduce(f32[4]{0:T(128)S(1)} %dynamic_update_slice.3, f32[2]{0:T(128)S(1)} %get-tuple-element.3, f32[2]{0:T(128)S(1)} %get-tuple-element.2), channel_id=1, replica_groups=mesh['domain'=2,'fsdp'=16] {'domain','fsdp'}, use_global_device_ids=true, to_apply=%region_5.6 | all-reduce | flops 8 | bytes 64 | tf_op jit(solution)/shard_map/psum | solution.py:55
  62.4 19.5 %all_to_all.23 = bf16[16,1,32,512]{3,2,1,0:T(8,128)(2,1)S(1)} all-to-all(bf16[16,1,32,512]{3,2,1,0:T(8,128)(2,1)S(1)} %divide_convert_fusion), channel_id=1, replica_groups=mesh['domain'=2,'fsdp'=16] {'fsdp'}, dimensions={0} | all-to-all | bytes 1048576 | tf_op jit(solution)/shard_map/all_to_all | solution.py:99
  82.6 2.5 collective-permute-done
  85.3 1.1 collective-permute-start.1
  86.4 24.2 %collective-permute-done.1 = f32[512,512]{1,0:T(8,128)S(1)} collective-permute-done((f32[512,512]{1,0:T(8,128)S(1)}, f32[512,512]{1,0:T(8,128)S(1)}, u32[]{:S(2)}, u32[]{:S(2)}) %collective-permute-start.1) | collective-permute-done | bytes 1048608 | tf_op jit(solution)/shard_map/ppermute | solution.py:17
  110.8 1.8 collective-permute-start.2
  112.6 22.8 %collective-permute-done.2 = f32[512,512]{1,0:T(8,128)S(1)} collective-permute-done((f32[512,512]{1,0:T(8,128)S(1)}, f32[512,512]{1,0:T(8,128)S(1)}, u32[]{:S(2)}, u32[]{:S(2)}) %collective-permute-start.2) | collective-permute-done | bytes 1048608 | tf_op jit(solution)/shard_map/ppermute | solution.py:17
  137.0 2.6 collective-permute-done.3
  139.9 1.3 collective-permute-start.4
  141.2 23.9 %collective-permute-done.4 = f32[512,512]{1,0:T(8,128)S(1)} collective-permute-done((f32[512,512]{1,0:T(8,128)S(1)}, f32[512,512]{1,0:T(8,128)S(1)}, u32[]{:S(2)}, u32[]{:S(2)}) %collective-permute-start.4) | collective-permute-done | bytes 1048608 | tf_op jit(solution)/shard_map/ppermute | solution.py:17
  165.4 1.8 collective-permute-start.5
  167.2 22.6 %collective-permute-done.5 = f32[512,512]{1,0:T(8,128)S(1)} collective-permute-done((f32[512,512]{1,0:T(8,128)S(1)}, f32[512,512]{1,0:T(8,128)S(1)}, u32[]{:S(2)}, u32[]{:S(2)}) %collective-permute-start.5) | collective-permute-done | bytes 1048608 | tf_op jit(solution)/shard_map/ppermute | solution.py:17
  191.4 2.6 collective-permute-done.6
  194.2 1.3 collective-permute-start.7
  195.6 23.9 %collective-permute-done.7 = f32[512,512]{1,0:T(8,128)S(1)} collective-permute-done((f32[512,512]{1,0:T(8,128)S(1)}, f32[512,512]{1,0:T(8,128)S(1)}, u32[]{:S(2)}, u32[]{:S(2)}) %collective-permute-start.7) | collective-permute-done | bytes 1048608 | tf_op jit(solution)/shard_map/ppermute | solution.py:17
  219.7 1.8 collective-permute-start.8
  221.5 22.6 %collective-permute-done.8 = f32[512,512]{1,0:T(8,128)S(1)} collective-permute-done((f32[512,512]{1,0:T(8,128)S(1)}, f32[512,512]{1,0:T(8,128)S(1)}, u32[]{:S(2)}, u32[]{:S(2)}) %collective-permute-start.8) | collective-permute-done | bytes 1048608 | tf_op jit(solution)/shard_map/ppermute | solution.py:17
  255.0 4.4 %all-to-all-start.2 = ((bf16[16,1,1,32,512]{4,3,2,1,0:T(8,128)(2,1)}), bf16[16,1,1,32,512]{4,3,2,1,0:T(8,128)(2,1)S(1)}, u32[]{:S(2)}, u32[]{:S(2)}) async-start(bf16[16,1,1,32,512]{4,3,2,1,0:T(8,128)(2,1)} %constant_dynamic-update-slice_fusion), calls=%async_computation.2 | async-start | bytes 1048576 | tf_op jit(solution)/shard_map/all_to_all | solution.py:105
  259.5 1.3 fusion.21
  260.9 1.2 broadcast_divide_fusion
  262.1 11.6 %all-to-all-done.2 = bf16[16,1,1,32,512]{4,3,2,1,0:T(8,128)(2,1)S(1)} async-done(((bf16[16,1,1,32,512]{4,3,2,1,0:T(8,128)(2,1)}), bf16[16,1,1,32,512]{4,3,2,1,0:T(8,128)(2,1)S(1)}, u32[]{:S(2)}, u32[]{:S(2)}) %all-to-all-start.2) | async-done | bytes 524320 | tf_op jit(solution)/shard_map/all_to_all | solution.py:105
  273.7 1.1 convert_multiply_fusion
  (58 shorter events, 20.2 us)
Async XLA Ops:
  0.6 4.4 %copy-start.2 = (s32[2]{0:T(128)S(1)}, s32[2]{0:T(128)}, u32[]{:S(2)}) copy-start(s32[2]{0:T(128)} %param.6) | copy-start | bytes 28
  0.6 4.5 %copy-start = (f32[8]{0:T(128)S(1)}, f32[8]{0:T(128)}, u32[]{:S(2)}) copy-start(f32[8]{0:T(128)} %param.7) | copy-start | bytes 100
  0.7 5.1 %copy-start.1 = (s32[4]{0:T(128)S(1)}, s32[4]{0:T(128)}, u32[]{:S(2)}) copy-start(s32[4]{0:T(128)} %param.5) | copy-start | bytes 52
  0.7 18.8 %all-to-all-start = ((bf16[1,2,2,256,512]{4,3,2,0,1:T(8,128)(2,1)}), bf16[1,2,2,256,512]{4,3,2,0,1:T(8,128)(2,1)S(1)}, u32[]{:S(2)}, u32[]{:S(2)}) async-start(bf16[1,2,2,256,512]{4,3,2,0,1:T(8,128)(2,1)} %bitcast.93), calls=%async_computation | async-start | bytes 2097152 | tf_op jit(solution)/shard_map/all_to_all | solution.py:73
  82.4 2.7 collective-permute-start
  85.3 25.3 %collective-permute-start.1 = (f32[512,512]{1,0:T(8,128)S(1)}, f32[512,512]{1,0:T(8,128)S(1)}, u32[]{:S(2)}, u32[]{:S(2)}) collective-permute-start(f32[512,512]{1,0:T(8,128)S(1)} %add.76), channel_id=1, source_target_pairs={{0,2},{1,3},{2,0},{3,1},{4,6},{5,7},{6,4},{7,5},{8,10},{9,11},{10,... | collective-permute-start | bytes 3145736 | tf_op jit(solution)/shard_map/ppermute | solution.py:17
  110.8 24.7 %collective-permute-start.2 = (f32[512,512]{1,0:T(8,128)S(1)}, f32[512,512]{1,0:T(8,128)S(1)}, u32[]{:S(2)}, u32[]{:S(2)}) collective-permute-start(f32[512,512]{1,0:T(8,128)S(1)} %add.77), channel_id=1, source_target_pairs={{0,4},{1,5},{2,6},{3,7},{4,0},{5,1},{6,2},{7,3},{8,12},{9,13},{10,... | collective-permute-start | bytes 3145736 | tf_op jit(solution)/shard_map/ppermute | solution.py:17
  137.0 2.7 collective-permute-start.3
  139.9 25.3 %collective-permute-start.4 = (f32[512,512]{1,0:T(8,128)S(1)}, f32[512,512]{1,0:T(8,128)S(1)}, u32[]{:S(2)}, u32[]{:S(2)}) collective-permute-start(f32[512,512]{1,0:T(8,128)S(1)} %add.81), channel_id=1, source_target_pairs={{0,2},{1,3},{2,0},{3,1},{4,6},{5,7},{6,4},{7,5},{8,10},{9,11},{10,... | collective-permute-start | bytes 3145736 | tf_op jit(solution)/shard_map/ppermute | solution.py:17
  165.4 24.4 %collective-permute-start.5 = (f32[512,512]{1,0:T(8,128)S(1)}, f32[512,512]{1,0:T(8,128)S(1)}, u32[]{:S(2)}, u32[]{:S(2)}) collective-permute-start(f32[512,512]{1,0:T(8,128)S(1)} %add.82), channel_id=1, source_target_pairs={{0,4},{1,5},{2,6},{3,7},{4,0},{5,1},{6,2},{7,3},{8,12},{9,13},{10,... | collective-permute-start | bytes 3145736 | tf_op jit(solution)/shard_map/ppermute | solution.py:17
  191.3 2.7 collective-permute-start.6
  194.2 25.3 %collective-permute-start.7 = (f32[512,512]{1,0:T(8,128)S(1)}, f32[512,512]{1,0:T(8,128)S(1)}, u32[]{:S(2)}, u32[]{:S(2)}) collective-permute-start(f32[512,512]{1,0:T(8,128)S(1)} %add.86), channel_id=1, source_target_pairs={{0,2},{1,3},{2,0},{3,1},{4,6},{5,7},{6,4},{7,5},{8,10},{9,11},{10,... | collective-permute-start | bytes 3145736 | tf_op jit(solution)/shard_map/ppermute | solution.py:17
  219.7 24.4 %collective-permute-start.8 = (f32[512,512]{1,0:T(8,128)S(1)}, f32[512,512]{1,0:T(8,128)S(1)}, u32[]{:S(2)}, u32[]{:S(2)}) collective-permute-start(f32[512,512]{1,0:T(8,128)S(1)} %add.87), channel_id=1, source_target_pairs={{0,4},{1,5},{2,6},{3,7},{4,0},{5,1},{6,2},{7,3},{8,12},{9,13},{10,... | collective-permute-start | bytes 3145736 | tf_op jit(solution)/shard_map/ppermute | solution.py:17
  255.0 18.7 %all-to-all-start.2 = ((bf16[16,1,1,32,512]{4,3,2,1,0:T(8,128)(2,1)}), bf16[16,1,1,32,512]{4,3,2,1,0:T(8,128)(2,1)S(1)}, u32[]{:S(2)}, u32[]{:S(2)}) async-start(bf16[16,1,1,32,512]{4,3,2,1,0:T(8,128)(2,1)} %constant_dynamic-update-slice_fusion), calls=%async_computation.2 | async-start | bytes 1048576 | tf_op jit(solution)/shard_map/all_to_all | solution.py:105
